TPU v7x, 32 devices: a whole 2x2x4 slice. The times are simulated.
32 devices in a mesh: expert: 16 (over z, y, x), replica: 2 (over core).
Axes of the slice: x: 2, y: 2, z: 4, core: 2. Of those that a mesh axis runs over, the one named last changes fastest.
Arguments:
- tokens: bfloat16 [1024, 7168], P('expert', 'replica'), may hold values from -6 to 6
- routes: int32 [1024, 8], P('expert'), may hold values from 0 to 15, all different within a row; in each aligned block of 64 rows (0 to 63, 64 to 127, ...) at most 64 rows name the same one
- route_scores: float32 [1024, 8], P('expert'), may hold values from 0.05 to 1
- placement: int32 [16], replicated, may hold values from 0 to 15, each once
- w_in: bfloat16 [16, 7168, 2, 1024], P('expert', 'replica'), may hold values from -0.0625 to 0.0625
- w_out: bfloat16 [16, 1024, 7168], P('expert', None, 'replica'), may hold values from -0.1875 to 0.1875
Outputs:
- mixed: bfloat16 [1024, 7168], P('expert', 'replica')
Inputs may be any that keep to these rules, and one draw needn't show every extreme that they name: `routes`: each row names 8 different logical experts. Among the 64 rows of each aligned block (the tokens of one index of the expert axis) no expert is named by more than 64 rows, a bound that some block reaches. `placement`: A permutation of the physical slots.
All inputs are finite; a program needn't handle non-finite values.
Results may differ from a plain program's by a relative error of at most 0.0057.
Values may be sent and summed in bfloat16 or wider, within the bound.
A program may use at most 128 MiB of HBM per device.

v0:
```python
import jax
import jax.numpy as jnp
from jax import lax
from jax.sharding import PartitionSpec as P


def packed(tokens, routes, route_scores, placement, w_in, w_out):
    tok_rows, feature_cols = tokens.shape
    route_count = routes.shape[1]
    experts = placement.shape[0]
    hidden_units = w_in.shape[3]
    capacity = min(tok_rows, max(2, 2 * tok_rows * route_count // experts))
    slot_total = experts * capacity
    expert_ids = jnp.arange(experts, dtype=jnp.int32)
    route_table = routes[:, :, None] == expert_ids
    physical = jnp.sum(jnp.where(route_table, placement, 0), axis=-1)
    flat_slots = physical.reshape(-1)
    onehot = (flat_slots[:, None] == expert_ids).astype(jnp.int32)
    earlier = jnp.sum((jnp.cumsum(onehot, axis=0) - onehot) * onehot, axis=1)
    position = (flat_slots * capacity + earlier).reshape(tok_rows, route_count)
    slot_index = jnp.arange(slot_total, dtype=jnp.int32)
    placing = jnp.any(position[None, :, :] == slot_index[:, None, None], axis=-1).astype(
        jnp.bfloat16
    )
    outgoing = jnp.dot(placing, tokens, preferred_element_type=jnp.float32).astype(jnp.bfloat16)
    incoming = lax.all_to_all(outgoing, "expert", split_axis=0, concat_axis=0, tiled=True)
    weights_in = w_in[0].reshape(feature_cols, 2 * hidden_units)
    weights_out = w_out[0]
    partial_value = jnp.dot(incoming, weights_in, preferred_element_type=jnp.float32)
    partial_value = partial_value.reshape(slot_total, 2, hidden_units)
    shares = lax.psum_scatter(partial_value, "replica", scatter_dimension=2, tiled=True)
    active = (jax.nn.silu(shares[:, 0]) * shares[:, 1]).astype(jnp.bfloat16)
    result = jnp.dot(
        lax.all_gather(active, "replica", axis=1, tiled=True),
        weights_out,
        preferred_element_type=jnp.float32,
    )
    expert_out = result.astype(jnp.bfloat16)
    returned = lax.all_to_all(expert_out, "expert", split_axis=0, concat_axis=0, tiled=True)
    route_weight = 2.5 * route_scores / jnp.sum(route_scores, axis=1, keepdims=True)
    picked = returned[position.reshape(-1)].reshape(tok_rows, route_count, feature_cols)
    mixed = jnp.sum(picked.astype(jnp.float32) * route_weight[:, :, None], axis=1)
    return mixed.astype(jnp.bfloat16)


def expert_weights(routes, route_scores, placement):
    experts = placement.shape[0]
    expert_ids = jnp.arange(experts, dtype=jnp.int32)
    physical = jnp.sum(jnp.where(routes[:, :, None] == expert_ids, placement, 0), axis=-1)
    route_weight = 2.5 * route_scores / jnp.sum(route_scores, axis=1, keepdims=True)
    return jnp.sum(
        jnp.where(physical[:, :, None] == expert_ids, route_weight[:, :, None], 0.0), axis=1
    )


def dense(tokens, routes, route_scores, placement, w_in, w_out):
    feature_cols = tokens.shape[1]
    hidden_units = w_in.shape[3]
    table = expert_weights(routes, route_scores, placement)
    mine = lax.all_to_all(table, "expert", split_axis=1, concat_axis=0, tiled=True)
    incoming = lax.all_gather(tokens, "expert", axis=0, tiled=True)
    rows = incoming.shape[0]
    weights_in = w_in[0].reshape(feature_cols, 2 * hidden_units)
    partial_value = jnp.dot(incoming, weights_in, preferred_element_type=jnp.float32)
    partial_value = partial_value.reshape(rows, 2, hidden_units)
    shares = lax.psum_scatter(partial_value, "replica", scatter_dimension=2, tiled=True)
    active = (jax.nn.silu(shares[:, 0]) * shares[:, 1]).astype(jnp.bfloat16)
    result = jnp.dot(
        lax.all_gather(active, "replica", axis=1, tiled=True),
        w_out[0],
        preferred_element_type=jnp.float32,
    )
    weighted = (result.astype(jnp.bfloat16).astype(jnp.float32) * mine).astype(jnp.bfloat16)
    return lax.psum_scatter(weighted, "expert", scatter_dimension=0, tiled=True)


def on_device(tokens, routes, route_scores, placement, w_in, w_out):
    tok_rows = tokens.shape[0]
    if 2 * tok_rows * routes.shape[1] // placement.shape[0] >= tok_rows:
        return dense(tokens, routes, route_scores, placement, w_in, w_out)
    return packed(tokens, routes, route_scores, placement, w_in, w_out)


def solution(mesh):
    in_specs = (
        P("expert", "replica"),
        P("expert", None),
        P("expert", None),
        P(),
        P("expert", "replica", None, None),
        P("expert", None, "replica"),
    )
    out_specs = P("expert", "replica")
    return jax.shard_map(
        on_device, mesh=mesh, in_specs=in_specs, out_specs=out_specs, check_vma=False
    )
```

profile of v0, /device:TPU:10, one launch (start us, length us, event | category | flops | bytes accessed | tf_op | source)
XLA Modules:
  0.0 345.8 jit_solution(17655661760736529164)
XLA Ops:
  6.5 0.0 all-gather.3.cloned.1.call-start
  6.5 0.7 all-gather.3.cloned.1.call-update
  7.3 0.0 reduce-scatter.3.cloned.1.call-start
  7.3 16.1 %copy.18 = bf16[448,8,2,1024]{3,1,2,0:T(8,128)(2,1)} copy(bf16[448,8,2,1024]{3,2,1,0:T(2,128)(2,1)} %bitcast.32) | data formatting | bytes 29360128
  23.4 18.9 %copy.16 = bf16[2048,3584]{1,0:T(8,128)(2,1)} copy(bf16[2048,3584]{0,1:T(8,128)(2,1)} %bitcast.31) | data formatting | bytes 29360128 | tf_op jit(solution)/shard_map/dot_general | solution.py:64
  42.3 71.1 %all-gather.3.cloned.1.call-done = bf16[1024,3584]{1,0:T(8,128)(2,1)} async-done(((bf16[64,3584]{1,0:T(8,128)(2,1)}), bf16[1024,3584]{1,0:T(8,128)(2,1)}) %all-gather.3.cloned.1.call-update) | async-done | bytes 7340048 | tf_op jit(solution)/shard_map/all_gather | solution.py:61
  113.4 21.6 %fusion.3 = f32[1024,2,1024]{2,0,1:T(8,128)} fusion(bf16[2,1024,3584]{2,1,0:T(8,128)(2,1)} %bitcast.33, bf16[1024,3584]{1,0:T(8,128)(2,1)} %all-gather.3.cloned.1.call-done), kind=kOutput, calls=%fused_computation.3 | convolution fusion | flops 15032385536 | bytes 30408704 | tf_op jit(solution)/shard_map/dot_general | solution.py:64
  135.0 0.0 copy-start
  135.0 0.0 copy-start.1
  135.0 0.0 reduce-scatter.3.cloned.1.call-update
  135.0 0.0 all-gather.5.cloned.1.call-start
  135.0 15.7 %reduce-scatter.3.cloned.1.call-done = f32[1024,2,512]{2,0,1:T(8,128)} async-done(((f32[1024,2,1024]{2,0,1:T(8,128)}), f32[1024,2,512]{2,0,1:T(8,128)}) %reduce-scatter.3.cloned.1.call-update) | async-done | bytes 4194320 | tf_op jit(solution)/shard_map/reduce_scatter | solution.py:66
  150.7 3.8 %fusion.6 = bf16[1024,512]{1,0:T(8,128)(2,1)} fusion(f32[1024,2,512]{2,0,1:T(8,128)} %reduce-scatter.3.cloned.1.call-done), kind=kLoop, calls=%fused_computation.7 | loop fusion | flops 3145728 | bytes 5242880 | tf_op jit(solution)/shard_map/convert_element_type | solution.py:67
  154.5 0.0 all-gather.5.cloned.1.call-update
  154.6 0.0 reduce-scatter.5.cloned.1.call-start
  154.6 0.0 copy-done
  154.7 0.0 copy-done.1
  154.7 0.0 copy-done.2
  154.7 0.1 select_reduce_fusion.1
  154.8 11.8 %all_to_all.16 = f32[64,16,1]{0,2,1:T(1,128)S(1)} all-to-all(f32[64,16,1]{0,2,1:T(1,128)S(1)} %bitcast.34), channel_id=1, replica_groups=mesh['expert'=16,'replica'=2] {'expert'}, dimensions={1} | all-to-all | bytes 8192 | tf_op jit(solution)/shard_map/all_to_all | solution.py:60
  166.7 0.1 mul.27
  166.7 12.5 %multiply_convert_fusion = bf16[1024,3584]{1,0:T(8,128)(2,1)} fusion(bf16[1024,1024]{1,0:T(8,128)(2,1)} %all-gather.5.cloned.1.call-done, bf16[1,1024,3584]{2,1,0:T(8,128)(2,1)} %param.11, f32[1024]{0:T(1024)S(1)} %mul.27), kind=kOutput, calls=%fused_computation | convolution fusion | flops 7530872832 | bytes 16781312 | tf_op jit(solution)/shard_map/dot_general | solution.py:68
  179.2 0.0 reduce-scatter.5.cloned.1.call-update
  179.3 160.0 %reduce-scatter.5.cloned.1.call-done = bf16[64,3584]{1,0:T(8,128)(2,1)} async-done(((bf16[1024,3584]{1,0:T(8,128)(2,1)}), bf16[64,3584]{1,0:T(8,128)(2,1)}) %reduce-scatter.5.cloned.1.call-update) | async-done | bytes 458768 | tf_op jit(solution)/shard_map/reduce_scatter | solution.py:74
  (6 shorter events, 0.1 us)
Async XLA Ops:
  6.5 106.8 %all-gather.3.cloned.1.call-start = ((), (), s32[]{:S(2)}) async-start(), calls=%async_computation.3 | async-start | bytes 7798784 | tf_op jit(solution)/shard_map/all_gather | solution.py:61
  7.3 143.4 %reduce-scatter.3.cloned.1.call-start = ((), (), s32[]{:S(2)}) async-start(), calls=%async_computation.4 | async-start | bytes 12582912 | tf_op jit(solution)/shard_map/reduce_scatter | solution.py:66
  135.0 19.7 %copy-start = (f32[64,8]{0,1:T(8,128)S(1)}, f32[64,8]{0,1:T(8,128)}, u32[]{:S(2)}) copy-start(f32[64,8]{0,1:T(8,128)} %param.8) | copy-start | bytes 6148
  135.0 19.7 %copy-start.1 = (s32[64,8]{0,1:T(8,128)S(1)}, s32[64,8]{0,1:T(8,128)}, u32[]{:S(2)}) copy-start(s32[64,8]{0,1:T(8,128)} %param.7) | copy-start | bytes 6148
  135.0 19.7 %copy-start.2 = (s32[16]{0:T(128)S(1)}, s32[16]{0:T(128)}, u32[]{:S(2)}) copy-start(s32[16]{0:T(128)} %param.9) | copy-start | bytes 196
  135.0 31.7 %all-gather.5.cloned.1.call-start = ((), (), s32[]{:S(2)}) async-start(), calls=%async_computation.5 | async-start | bytes 3145728 | tf_op jit(solution)/shard_map/all_gather | solution.py:69
  154.6 184.7 %reduce-scatter.5.cloned.1.call-start = ((), (), s32[]{:S(2)}) async-start(), calls=%async_computation.6 | async-start | bytes 7798784 | tf_op jit(solution)/shard_map/reduce_scatter | solution.py:74
Sparse Core Ops, SparseCore 0:
  10.0 103.2 all-gather.2
  135.1 15.5 reduce-scatter.2
  154.7 11.7 all-gather.4
  179.4 159.8 reduce-scatter.4
where the time goes:
time: 347 us; the launch traced here: 346 us
  waiting for transfers between devices  248 us (71%)
  local copies, waits for them, and re-layouts  35.1 us (10%)
  matrix products  34.1 us (10%)
  between operations  13.2 us (4%)
  blocking collectives  11.8 us (3%)
  other arithmetic  3.98 us (1%)
    reduce_scatter x1, waiting for transfers between devices, dense(): return lax.psum_scatter(weighted, 'expert', scatter_dimension=0, tiled=True)  160 us
    all_gather x1, waiting for transfers between devices, dense(): incoming = lax.all_gather(tokens, 'expert', axis=0, tiled=True)  71.1 us
    dot_general x1, matrix products, dense(): jnp.dot(incoming, weights_in, preferred_element_type=jnp.float32)  21.6 us
    dot_general x1, local copies, waits for them, and re-layouts, dense(): jnp.dot(incoming, weights_in, preferred_element_type=jnp.float32)  18.9 us
    unnamed x7, local copies, waits for them, and re-layouts  16.1 us
    reduce_scatter x1, waiting for transfers between devices, dense(): lax.psum_scatter(partial_value, 'replica', scatter_dimension=2, tiled=True)  15.7 us
    dot_general x1, matrix products, dense(): jnp.dot(lax.all_gather(active, 'replica', axis=1, tiled=True), w_out[0],...  12.5 us
    all_to_all x1, blocking collectives, dense(): lax.all_to_all(table, 'expert', split_axis=1, concat_axis=0, tiled=True)  11.8 us
  transfers between devices with their start and end apart: 4, of which 3 were waited for; matrix products, arithmetic and copies ran while one was open for 10% of the time, Pallas kernels for 0%

commit v1 on v0

--- a/solution.py
+++ b/solution.py
@@ -58,7 +58,14 @@
     hidden_units = w_in.shape[3]
     table = expert_weights(routes, route_scores, placement)
     mine = lax.all_to_all(table, "expert", split_axis=1, concat_axis=0, tiled=True)
-    incoming = lax.all_gather(tokens, "expert", axis=0, tiled=True)
+    ways, here = (lax.axis_size("expert"), lax.axis_index("expert"))
+    incoming, reach = (tokens, 1)
+    while reach < ways:
+        theirs = lax.ppermute(incoming, "expert", [(d, d ^ reach) for d in range(ways)])
+        mine_first = jnp.concatenate([incoming, theirs], axis=0)
+        theirs_first = jnp.concatenate([theirs, incoming], axis=0)
+        incoming = jnp.where(here & reach == 0, mine_first, theirs_first)
+        reach = 2 * reach
     rows = incoming.shape[0]
     weights_in = w_in[0].reshape(feature_cols, 2 * hidden_units)
     partial_value = jnp.dot(incoming, weights_in, preferred_element_type=jnp.float32)

time: 347 us -> 485 us (1.40)
  waiting for transfers between devices: 248 us -> 370 us
  other arithmetic: 3.98 us -> 11.1 us
  starting transfers between devices: 0.12 us -> 5.31 us
    ppermute x0 -> x4, waiting for transfers between devices: none -> 192 us  [dense(): lax.ppermute(incoming, 'expert', [(d, d ^ reach) for d in range(ways)])]
    all_gather x1 -> x0, waiting for transfers between devices: 71.1 us -> none  [dense(): incoming = lax.all_gather(tokens, 'expert', axis=0, tiled=True)]
    select_n x0 -> x3, other arithmetic: none -> 7.08 us  [dense(): incoming = jnp.where(here & reach == 0, mine_first, theirs_first)]
    ppermute x0 -> x4, starting transfers between devices: none -> 5.22 us  [dense(): lax.ppermute(incoming, 'expert', [(d, d ^ reach) for d in range(ways)])]
  transfers between devices with their start and end apart: 4 -> 7, of which waited for: 3 -> 6; matrix products, arithmetic and copies ran while one was open for 10% -> 7% of each run, Pallas kernels for 0% -> 0%
where the time goes in v1:
time: 485 us; the launch traced here: 484 us
  waiting for transfers between devices  370 us (76%)
  matrix products  37.3 us (8%)
  local copies, waits for them, and re-layouts  34.9 us (7%)
  between operations  13.2 us (3%)
  blocking collectives  11.8 us (2%)
  other arithmetic  11.1 us (2%)
  starting transfers between devices  5.31 us (1%)
    ppermute x4, waiting for transfers between devices, dense(): lax.ppermute(incoming, 'expert', [(d, d ^ reach) for d in range(ways)])  192 us
    reduce_scatter x1, waiting for transfers between devices, dense(): return lax.psum_scatter(weighted, 'expert', scatter_dimension=0, tiled=True)  160 us
    dot_general x1, matrix products, dense(): jnp.dot(incoming, weights_in, preferred_element_type=jnp.float32)  24.8 us
    dot_general x1, local copies, waits for them, and re-layouts, dense(): jnp.dot(incoming, weights_in, preferred_element_type=jnp.float32)  18.8 us
    reduce_scatter x1, waiting for transfers between devices, dense(): lax.psum_scatter(partial_value, 'replica', scatter_dimension=2, tiled=True)  18.6 us
    unnamed x7, local copies, waits for them, and re-layouts  16 us
    dot_general x1, matrix products, dense(): jnp.dot(lax.all_gather(active, 'replica', axis=1, tiled=True), w_out[0],...  12.5 us
    all_to_all x1, blocking collectives, dense(): lax.all_to_all(table, 'expert', split_axis=1, concat_axis=0, tiled=True)  11.8 us
  transfers between devices with their start and end apart: 7, of which 6 were waited for; matrix products, arithmetic and copies ran while one was open for 7% of the time, Pallas kernels for 0%

profile of v1, /device:TPU:10, one launch (start us, length us, event | category | flops | bytes accessed | tf_op | source)
XLA Modules:
  0.0 483.8 jit_solution(5600653667757588298)
XLA Ops:
  6.5 0.5 collective-permute-start
  7.1 11.9 %collective-permute-done = bf16[64,3584]{1,0:T(8,128)(2,1)S(1)} collective-permute-done((bf16[64,3584]{1,0:T(8,128)(2,1)}, bf16[64,3584]{1,0:T(8,128)(2,1)S(1)}, u32[]{:S(2)}, u32[]{:S(2)}) %collective-permute-start) | collective-permute-done | bytes 458784 | tf_op jit(solution)/shard_map/ppermute | solution.py:64
  19.0 1.3 maximum_select_fusion.3
  20.3 1.6 collective-permute-start.1
  21.9 19.8 %collective-permute-done.1 = bf16[128,3584]{1,0:T(8,128)(2,1)} collective-permute-done((bf16[128,3584]{1,0:T(8,128)(2,1)S(1)}, bf16[128,3584]{1,0:T(8,128)(2,1)}, u32[]{:S(2)}, u32[]{:S(2)}) %collective-permute-start.1) | collective-permute-done | bytes 917536 | tf_op jit(solution)/shard_map/ppermute | solution.py:64
  41.8 1.9 maximum_select_fusion.2
  43.7 0.5 collective-permute-start.2
  44.2 39.7 %collective-permute-done.2 = bf16[256,3584]{1,0:T(8,128)(2,1)} collective-permute-done((bf16[256,3584]{1,0:T(8,128)(2,1)S(1)}, bf16[256,3584]{1,0:T(8,128)(2,1)}, u32[]{:S(2)}, u32[]{:S(2)}) %collective-permute-start.2) | collective-permute-done | bytes 1835040 | tf_op jit(solution)/shard_map/ppermute | solution.py:64
  83.9 3.9 maximum_select_fusion.1
  87.7 2.6 collective-permute-start.3
  90.3 16.0 %copy.18 = bf16[448,8,2,1024]{3,1,2,0:T(8,128)(2,1)} copy(bf16[448,8,2,1024]{3,2,1,0:T(2,128)(2,1)} %bitcast.32) | data formatting | bytes 29360128
  106.3 18.8 %copy.16 = bf16[2048,3584]{1,0:T(8,128)(2,1)} copy(bf16[2048,3584]{0,1:T(8,128)(2,1)} %bitcast.31) | data formatting | bytes 29360128 | tf_op jit(solution)/shard_map/dot_general | solution.py:71
  125.1 120.1 %collective-permute-done.3 = bf16[512,3584]{1,0:T(8,128)(2,1)} collective-permute-done((bf16[512,3584]{1,0:T(8,128)(2,1)}, bf16[512,3584]{1,0:T(8,128)(2,1)}, u32[]{:S(2)}, u32[]{:S(2)}) %collective-permute-start.3) | collective-permute-done | bytes 3670048 | tf_op jit(solution)/shard_map/ppermute | solution.py:64
  245.2 24.8 %fusion.1 = f32[1024,2,1024]{2,0,1:T(8,128)} fusion(bf16[2,1024,3584]{2,1,0:T(8,128)(2,1)} %bitcast.33, bf16[512,3584]{1,0:T(8,128)(2,1)} %collective-permute-done.3, bf16[512,3584]{1,0:T(8,128)(2,1)} %maximum_select_fusion.1, pred[]{:T(512)S(6)} %eq.38), kind=kOutput, calls=%fused_computation.4 | convolution fusion | flops 15065415680 | bytes 30408704 | tf_op jit(solution)/shard_map/dot_general | solution.py:71
  270.0 0.0 reduce-scatter.3.cloned.1.call-update
  270.0 0.0 all-gather.2.cloned.1.call-start
  270.1 18.6 %reduce-scatter.3.cloned.1.call-done = f32[1024,2,512]{2,0,1:T(8,128)} async-done(((f32[1024,2,1024]{2,0,1:T(8,128)}), f32[1024,2,512]{2,0,1:T(8,128)}) %reduce-scatter.3.cloned.1.call-update) | async-done | bytes 4194320 | tf_op jit(solution)/shard_map/reduce_scatter | solution.py:73
  288.7 3.8 fusion.13
  292.6 0.0 reduce-scatter.5.cloned.1.call-start
  292.6 0.1 select_reduce_fusion.1
  292.8 11.8 %all_to_all.16 = f32[64,16,1]{0,2,1:T(1,128)S(1)} all-to-all(f32[64,16,1]{0,2,1:T(1,128)S(1)} %bitcast.34), channel_id=1, replica_groups=mesh['expert'=16,'replica'=2] {'expert'}, dimensions={1} | all-to-all | bytes 8192 | tf_op jit(solution)/shard_map/all_to_all | solution.py:60
  304.6 0.1 mul.27
  304.7 12.5 %multiply_convert_fusion = bf16[1024,3584]{1,0:T(8,128)(2,1)} fusion(bf16[1024,1024]{1,0:T(8,128)(2,1)} %all-gather.2.cloned.1.call-done, bf16[1,1024,3584]{2,1,0:T(8,128)(2,1)} %param.11, f32[1024]{0:T(1024)S(1)} %mul.27), kind=kOutput, calls=%fused_computation | convolution fusion | flops 7530872832 | bytes 16781312 | tf_op jit(solution)/shard_map/dot_general | solution.py:75
  317.2 160.0 %reduce-scatter.5.cloned.1.call-done = bf16[64,3584]{1,0:T(8,128)(2,1)} async-done(((bf16[1024,3584]{1,0:T(8,128)(2,1)}), bf16[64,3584]{1,0:T(8,128)(2,1)}) %reduce-scatter.5.cloned.1.call-update) | async-done | bytes 458768 | tf_op jit(solution)/shard_map/reduce_scatter | solution.py:81
  (14 shorter events, 0.1 us)
Async XLA Ops:
  6.5 282.1 %reduce-scatter.3.cloned.1.call-start = ((), (), s32[]{:S(2)}) async-start(), calls=%async_computation.3 | async-start | bytes 12582912 | tf_op jit(solution)/shard_map/reduce_scatter | solution.py:73
  6.5 12.5 %collective-permute-start = (bf16[64,3584]{1,0:T(8,128)(2,1)}, bf16[64,3584]{1,0:T(8,128)(2,1)S(1)}, u32[]{:S(2)}, u32[]{:S(2)}) collective-permute-start(bf16[64,3584]{1,0:T(8,128)(2,1)} %param.6), channel_id=1, source_target_pairs={{0,2},{2,0},{4,6},{6,4},{8,10},{10,8},{12,14},{14,12},{16,18},{18,... | collective-permute-start | bytes 1376264 | tf_op jit(solution)/shard_map/ppermute | solution.py:64
  20.3 21.4 %collective-permute-start.1 = (bf16[128,3584]{1,0:T(8,128)(2,1)S(1)}, bf16[128,3584]{1,0:T(8,128)(2,1)}, u32[]{:S(2)}, u32[]{:S(2)}) collective-permute-start(bf16[128,3584]{1,0:T(8,128)(2,1)S(1)} %maximum_select_fusion.3), channel_id=1, source_target_pairs={{0,4},{2,6},{4,0},{6,2},{8,12},{10,14},{12,8},{14,10},{16,20},{18,... | collective-permute-start | bytes 2752520 | tf_op jit(solution)/shard_map/ppermute | solution.py:64
  43.7 40.2 %collective-permute-start.2 = (bf16[256,3584]{1,0:T(8,128)(2,1)S(1)}, bf16[256,3584]{1,0:T(8,128)(2,1)}, u32[]{:S(2)}, u32[]{:S(2)}) collective-permute-start(bf16[256,3584]{1,0:T(8,128)(2,1)S(1)} %maximum_select_fusion.2), channel_id=1, source_target_pairs={{0,8},{2,10},{4,12},{6,14},{8,0},{10,2},{12,4},{14,6},{16,24},{18,... | collective-permute-start | bytes 5505032 | tf_op jit(solution)/shard_map/ppermute | solution.py:64
  87.7 157.5 %collective-permute-start.3 = (bf16[512,3584]{1,0:T(8,128)(2,1)}, bf16[512,3584]{1,0:T(8,128)(2,1)}, u32[]{:S(2)}, u32[]{:S(2)}) collective-permute-start(bf16[512,3584]{1,0:T(8,128)(2,1)} %maximum_select_fusion.1), channel_id=1, source_target_pairs={{0,16},{2,18},{4,20},{6,22},{8,24},{10,26},{12,28},{14,30},{16,0},... | collective-permute-start | bytes 11010056 | tf_op jit(solution)/shard_map/ppermute | solution.py:64
  270.0 22.6 %copy-start = (f32[64,8]{0,1:T(8,128)S(1)}, f32[64,8]{0,1:T(8,128)}, u32[]{:S(2)}) copy-start(f32[64,8]{0,1:T(8,128)} %param.8) | copy-start | bytes 6148
  270.0 22.6 %copy-start.1 = (s32[64,8]{0,1:T(8,128)S(1)}, s32[64,8]{0,1:T(8,128)}, u32[]{:S(2)}) copy-start(s32[64,8]{0,1:T(8,128)} %param.7) | copy-start | bytes 6148
  270.0 22.6 %copy-start.2 = (s32[16]{0:T(128)S(1)}, s32[16]{0:T(128)}, u32[]{:S(2)}) copy-start(s32[16]{0:T(128)} %param.9) | copy-start | bytes 196
  270.0 34.7 %all-gather.2.cloned.1.call-start = ((), (), s32[]{:S(2)}) async-start(), calls=%async_computation.4 | async-start | bytes 3145728 | tf_op jit(solution)/shard_map/all_gather | solution.py:76
  292.6 184.7 %reduce-scatter.5.cloned.1.call-start = ((), (), s32[]{:S(2)}) async-start(), calls=%async_computation.5 | async-start | bytes 7798784 | tf_op jit(solution)/shard_map/reduce_scatter | solution.py:81
Sparse Core Ops, SparseCore 0:
  270.1 18.5 reduce-scatter.2
  292.7 11.7 all-gather.1
  317.4 159.8 reduce-scatter.4
